TPU v7x, 256 devices: a whole 4x4x8 slice. The times are simulated.
256 devices in a mesh: gz: 128 (over x, z_hi, y, core), ga: 2 (over z_lo).
Axes of the slice: x: 4, y: 4, z: 8 (z_hi: 4, z_lo: 2; z = z_hi * 2 + z_lo), core: 2. Of those that a mesh axis runs over, the one named last changes fastest.
Arguments:
- fractions: float32 [16, 512, 128, 128], P('ga', 'gz'), may hold values from 0.05 to 1
- courant: float32 [16], replicated, may hold values from -0.9 to 0.9, as said below
- spread: float32 [16], replicated, may hold values from 0.05 to 0.25
- inlet_frac: float32 [16], replicated, may hold values from 0.2 to 1
- flags: int32 [512, 128, 128], P('gz'), may hold values from 0 to 7
- table_index: int32 [512, 128], P('gz'), may hold values from 0 to 31
- lin_table: float32 [32, 16, 16], replicated, may hold values from -1.5 to 1.5
- quad_table: float32 [32, 16, 16], replicated, may hold values from -0.9 to 0.9
Outputs:
- updated: float32 [16, 512, 128, 128], P('ga', 'gz')
Inputs may be any that keep to these rules, and one draw needn't show every extreme that they name: Among groups 0 to 7, and in each further run of 8 groups, half have positive and half negative courant; magnitudes lie between 0.3 and 0.9.
All inputs are finite; a program needn't handle non-finite values.
Results may differ from a plain program's by a relative error of at most 0.00007.
Values sent between devices are 32-bit elements; how exact they have to be, the bound alone decides.
No kernel may reach another device: no remote copies, remote signals or barrier semaphores. Data moves between devices by JAX's collectives and lax.ppermute only.
A program may use at most 64 MiB of HBM per device.

v0:
```python
import jax
import jax.numpy as jnp
from jax import lax
from jax.sharding import PartitionSpec as P


def padded(block, sides, width):
    for axis, dim in sides:
        count = lax.axis_size(axis)
        forward = [(i, i + 1) for i in range(count - 1)]
        backward = [(target, source) for source, target in forward]
        low = lax.ppermute(
            lax.slice_in_dim(block, block.shape[dim] - width, None, axis=dim), axis, forward
        )
        high = lax.ppermute(lax.slice_in_dim(block, 0, width, axis=dim), axis, backward)
        block = jnp.concatenate([low, block, high], axis=dim)
    return block


def advect(ext, courant, spread, inlet_frac, flags):
    lower2 = ext[:, :-4]
    lower1 = ext[:, 1:-3]
    centre = ext[:, 2:-2]
    upper1 = ext[:, 3:-1]
    upper2 = ext[:, 4:]
    pos = jnp.maximum(courant, 0.0)[:, None, None, None]
    neg = jnp.minimum(courant, 0.0)[:, None, None, None]
    disp = spread[:, None, None, None]
    moved = centre - pos * 0.5 * (3.0 * centre - 4.0 * lower1 + lower2)
    moved = moved + pos * pos * 0.5 * (centre - 2.0 * lower1 + lower2)
    moved = moved - neg * 0.5 * (-3.0 * centre + 4.0 * upper1 - upper2)
    moved = moved + neg * neg * 0.5 * (centre - 2.0 * upper1 + upper2)
    moved = moved + disp * (upper1 - 2.0 * centre + lower1)
    moved = jnp.where(flags[None] == 2, jnp.float32(0.0), moved)
    moved = jnp.where(
        flags[None] == 1, inlet_frac[:, None, None, None] * jnp.ones_like(moved), moved
    )
    return moved


def regroup(blocks, table_index, lin_table, quad_table):
    groups, planes, nblk, width = blocks.shape
    ntables = lin_table.shape[0]
    onehot = (
        table_index.reshape(planes * nblk)[:, None] == jnp.arange(ntables, dtype=jnp.int32)[None, :]
    ).astype(jnp.float32)
    tables = jnp.concatenate([lin_table, quad_table], axis=1).reshape(ntables, 2 * groups * groups)
    picked = jnp.dot(
        onehot, tables, precision=lax.Precision.HIGHEST, preferred_element_type=jnp.float32
    )
    coeffs = picked.reshape(planes, nblk, 2 * groups, groups)
    applied = lax.dot_general(
        coeffs,
        blocks,
        (((3,), (0,)), ((0, 1), (1, 2))),
        precision=lax.Precision.HIGHEST,
        preferred_element_type=jnp.float32,
    )
    applied = jnp.transpose(applied, (2, 0, 1, 3))
    lin_part = applied[:groups]
    quad_part = applied[groups:]
    return blocks + 0.25 * (lin_part + blocks * quad_part)


def body(fractions, courant, spread, inlet_frac, flags, table_index, lin_table, quad_table):
    member = lax.axis_index("ga")
    local_groups = fractions.shape[0]
    half_blocks = fractions.shape[2] // lax.axis_size("ga")
    start_group = member * local_groups
    own_courant = lax.dynamic_slice_in_dim(courant, start_group, local_groups)
    own_spread = lax.dynamic_slice_in_dim(spread, start_group, local_groups)
    own_inlet = lax.dynamic_slice_in_dim(inlet_frac, start_group, local_groups)
    half_index = lax.dynamic_slice_in_dim(table_index, member * half_blocks, half_blocks, 1)
    extended = padded(fractions, (("gz", 1),), 2)
    first = advect(extended, own_courant, own_spread, own_inlet, flags)
    cell_view = lax.all_to_all(first, "ga", split_axis=2, concat_axis=0, tiled=True)
    second = regroup(cell_view, half_index, lin_table, quad_table)
    grouped = lax.all_to_all(second, "ga", split_axis=0, concat_axis=2, tiled=True)
    widened = padded(grouped, (("gz", 1),), 2)
    third = advect(widened, own_courant, own_spread, own_inlet, flags)
    again = lax.all_to_all(third, "ga", split_axis=2, concat_axis=0, tiled=True)
    fourth = regroup(again, half_index, lin_table, quad_table)
    return lax.all_to_all(fourth, "ga", split_axis=0, concat_axis=2, tiled=True)


def solution(mesh):
    placed = (
        P("ga", "gz", None, None),
        P(),
        P(),
        P(),
        P("gz", None, None),
        P("gz", None),
        P(),
        P(),
    )
    return jax.shard_map(
        body, mesh=mesh, in_specs=placed, out_specs=P("ga", "gz", None, None), check_vma=False
    )
```

profile of v0, /device:TPU:10, one launch (start us, length us, event | category | flops | bytes accessed | tf_op | source)
XLA Modules:
  0.0 187.8 jit_solution(8147574788965440206)
XLA Ops:
  0.0 3.1 %fusion.19 = (f32[8,2,128,128]{3,2,1,0:T(8,128)}, f32[8,2,128,128]{3,2,1,0:T(8,128)}) fusion(f32[8,4,128,128]{3,2,1,0:T(8,128)} %param.8), kind=kLoop, calls=%fused_computation.43 | loop fusion | bytes 4194304 | tf_op jit(solution)/shard_map/slice | solution.py:13
  3.2 2.0 %collective-permute-start = (f32[8,2,128,128]{3,2,1,0:T(8,128)}, f32[8,2,128,128]{3,2,1,0:T(8,128)}, u32[]{:S(2)}, u32[]{:S(2)}) collective-permute-start(f32[8,2,128,128]{3,2,1,0:T(8,128)} %get-tuple-element.11), channel_id=1, source_target_pairs={{0,2},{2,4},{4,6},{6,8},{8,10},{10,12},{12,14},{14,16},{16,18},{18... | collective-permute-start | bytes 3145736 | tf_op jit(solution)/shard_map/ppermute | solution.py:12
  5.2 3.6 %collective-permute-start.1 = (f32[8,2,128,128]{3,2,1,0:T(8,128)}, f32[8,2,128,128]{3,2,1,0:T(8,128)S(1)}, u32[]{:S(2)}, u32[]{:S(2)}) collective-permute-start(f32[8,2,128,128]{3,2,1,0:T(8,128)} %get-tuple-element.12), channel_id=1, source_target_pairs={{2,0},{4,2},{6,4},{8,6},{10,8},{12,10},{14,12},{16,14},{18,16},{20... | collective-permute-start | bytes 3145736 | tf_op jit(solution)/shard_map/ppermute | solution.py:15
  9.4 10.3 %collective-permute-done = f32[8,2,128,128]{3,2,1,0:T(8,128)} collective-permute-done((f32[8,2,128,128]{3,2,1,0:T(8,128)}, f32[8,2,128,128]{3,2,1,0:T(8,128)}, u32[]{:S(2)}, u32[]{:S(2)}) %collective-permute-start) | collective-permute-done | bytes 1048608 | tf_op jit(solution)/shard_map/ppermute | solution.py:12
  19.7 1.8 copy_dynamic-update-slice_fusion.3
  21.6 1.2 copy_dynamic-update-slice_fusion
  23.4 5.0 %select_select_fusion.1 = f32[8,4,128,128]{3,0,1,2:T(8,128)} fusion(f32[8,6,128,128]{3,0,1,2:T(8,128)S(1)} %copy_dynamic-update-slice_fusion.2, f32[8,6,128,128]{3,0,1,2:T(8,128)S(1)} %get-tuple-element.9, f32[8,4,128,128]{3,2,1,0:T(8,128)S(1)} %copy-done.1, f32[8]{0:T(128)S(1)} %dynamic_slice.14, f32[8]{0:T(128)S(1)} %get-tuple-element.16, ...), kind=kLoop, calls=%fused_computation.21 | loop fusion | flops 15204352 | bytes 12714176 | tf_op jit(solution)/shard_map/jit(_where)/select_n | solution.py:35
  28.4 5.1 %all-to-all-start = ((f32[8,4,128,128]{3,0,1,2:T(8,128)}), f32[8,4,128,128]{3,0,1,2:T(8,128)}, u32[]{:S(2)}, u32[]{:S(2)}) async-start(f32[8,4,128,128]{3,0,1,2:T(8,128)} %select_select_fusion.1), calls=%async_computation | async-start | bytes 4194304 | tf_op jit(solution)/shard_map/all_to_all | solution.py:76
  34.3 0.9 copy.57
  35.2 24.3 %all-to-all-done = f32[8,4,128,128]{3,0,1,2:T(8,128)} async-done(((f32[8,4,128,128]{3,0,1,2:T(8,128)}), f32[8,4,128,128]{3,0,1,2:T(8,128)}, u32[]{:S(2)}, u32[]{:S(2)}) %all-to-all-start) | async-done | bytes 2097184 | tf_op jit(solution)/shard_map/all_to_all | solution.py:76
  59.5 8.7 %convolution_bitcast_fusion.1 = f32[32,4,64,128]{3,0,2,1:T(8,128)S(1)} fusion(f32[4,64,32,16]{2,3,1,0:T(8,128)S(1)} %copy.57, f32[8,4,2,64,128]{4,0,1,3,2:T(8,128)} %bitcast), kind=kOutput, calls=%fused_computation.5 | convolution fusion | flops 201326592 | bytes 6815744 | tf_op jit(solution)/shard_map/dot_general | solution.py:52
  68.2 2.1 %fusion.7 = f32[16,4,64,128]{3,0,2,1:T(8,128)S(1)} fusion(f32[32,4,64,128]{3,0,2,1:T(8,128)S(1)} %convolution_bitcast_fusion.1, f32[8,4,2,64,128]{4,0,1,3,2:T(8,128)} %bitcast), kind=kLoop, calls=%fused_computation.17 | loop fusion | flops 2097152 | bytes 8388608 | tf_op jit(solution)/shard_map/add | solution.py:62
  70.3 0.7 copy.58
  71.0 27.7 %all_to_all.72 = f32[16,4,64,128]{3,2,1,0:T(8,128)S(1)} all-to-all(f32[16,4,64,128]{3,2,1,0:T(8,128)S(1)} %copy.58), channel_id=1, replica_groups=mesh['gz'=128,'ga'=2] {'ga'}, dimensions={0} | all-to-all | bytes 4194304 | tf_op jit(solution)/shard_map/all_to_all | solution.py:78
  98.7 1.2 copy.59
  100.4 1.9 %collective-permute-start.2 = (f32[8,2,128,128]{3,2,1,0:T(8,128)S(1)}, f32[8,2,128,128]{3,2,1,0:T(8,128)S(1)}, u32[]{:S(2)}, u32[]{:S(2)}) collective-permute-start(f32[8,2,128,128]{3,2,1,0:T(8,128)S(1)} %copy.60), channel_id=1, source_target_pairs={{0,2},{2,4},{4,6},{6,8},{8,10},{10,12},{12,14},{14,16},{16,18},{18... | collective-permute-start | bytes 3145736 | tf_op jit(solution)/shard_map/ppermute | solution.py:12
  102.6 3.9 %collective-permute-start.3 = (f32[8,2,128,128]{3,2,1,0:T(8,128)S(1)}, f32[8,2,128,128]{3,2,1,0:T(8,128)S(1)}, u32[]{:S(2)}, u32[]{:S(2)}) collective-permute-start(f32[8,2,128,128]{3,2,1,0:T(8,128)S(1)} %copy.62), channel_id=1, source_target_pairs={{2,0},{4,2},{6,4},{8,6},{10,8},{12,10},{14,12},{16,14},{18,16},{20... | collective-permute-start | bytes 3145736 | tf_op jit(solution)/shard_map/ppermute | solution.py:15
  106.5 10.0 %collective-permute-done.2 = f32[8,2,128,128]{3,2,1,0:T(8,128)S(1)} collective-permute-done((f32[8,2,128,128]{3,2,1,0:T(8,128)S(1)}, f32[8,2,128,128]{3,2,1,0:T(8,128)S(1)}, u32[]{:S(2)}, u32[]{:S(2)}) %collective-permute-start.2) | collective-permute-done | bytes 1048608 | tf_op jit(solution)/shard_map/ppermute | solution.py:12
  117.1 1.5 collective-permute-done.3
  119.2 2.6 %select_select_fusion = f32[8,4,128,128]{3,0,1,2:T(8,128)S(1)} fusion(f32[8,4,128,128]{3,0,1,2:T(8,128)S(1)} %bitcast.44, f32[8,2,128,128]{3,0,1,2:T(8,128)S(1)} %copy.63, f32[8,2,128,128]{3,0,1,2:T(8,128)S(1)} %copy.61, f32[8]{0:T(128)S(1)} %dynamic_slice.14, f32[8]{0:T(128)S(1)} %get-tuple-element.16, f32[8]{0:T(128)S(1)} %get-tuple-element.17, ...), kind=kLoop, calls=%fused_computation.20 | loop fusion | flops 17301504 | bytes 6422720 | tf_op jit(solution)/shard_map/jit(_where)/select_n | solution.py:35
  121.8 28.5 %all_to_all.73 = f32[8,4,128,128]{3,0,1,2:T(8,128)S(1)} all-to-all(f32[8,4,128,128]{3,0,1,2:T(8,128)S(1)} %select_select_fusion), channel_id=1, replica_groups=mesh['gz'=128,'ga'=2] {'ga'}, dimensions={2} | all-to-all | bytes 4194304 | tf_op jit(solution)/shard_map/all_to_all | solution.py:81
  150.3 7.1 %convolution_bitcast_fusion = f32[32,4,64,128]{3,0,2,1:T(8,128)S(1)} fusion(f32[4,64,32,16]{2,3,1,0:T(8,128)S(1)} %copy.57, f32[8,4,2,64,128]{4,0,1,3,2:T(8,128)S(1)} %bitcast.45), kind=kOutput, calls=%fused_computation.4 | convolution fusion | flops 201326592 | bytes 6815744 | tf_op jit(solution)/shard_map/dot_general | solution.py:52
  158.4 27.9 %all_to_all.74 = f32[16,4,64,128]{3,2,1,0:T(8,128)S(1)} all-to-all(f32[16,4,64,128]{3,2,1,0:T(8,128)S(1)} %copy.66), channel_id=1, replica_groups=mesh['gz'=128,'ga'=2] {'ga'}, dimensions={0} | all-to-all | bytes 4194304 | tf_op jit(solution)/shard_map/all_to_all | solution.py:83
  186.3 1.5 copy.67
  (35 shorter events, 4.9 us)
Async XLA Ops:
  0.0 33.6 %copy-start = (s32[4,128]{1,0:T(4,128)S(1)}, s32[4,128]{1,0:T(4,128)}, u32[]{:S(2)}) copy-start(s32[4,128]{1,0:T(4,128)} %param.13) | copy-start | bytes 6148
  0.0 8.9 %copy-start.2 = (s32[4,128,128]{2,1,0:T(8,128)S(1)}, s32[4,128,128]{2,1,0:T(8,128)}, u32[]{:S(2)}) copy-start(s32[4,128,128]{2,1,0:T(8,128)} %param.12) | copy-start | bytes 786436
  0.0 9.0 %copy-start.6 = (f32[16]{0:T(128)S(1)}, f32[16]{0:T(128)}, u32[]{:S(2)}) copy-start(f32[16]{0:T(128)} %param.11) | copy-start | bytes 196
  0.0 9.0 %copy-start.7 = (f32[16]{0:T(128)S(1)}, f32[16]{0:T(128)}, u32[]{:S(2)}) copy-start(f32[16]{0:T(128)} %param.10) | copy-start | bytes 196
  0.0 9.3 %copy-start.5 = (f32[16]{0:T(128)S(1)}, f32[16]{0:T(128)}, u32[]{:S(2)}) copy-start(f32[16]{0:T(128)} %param.9) | copy-start | bytes 196
  3.2 18.4 %copy-start.1 = (f32[8,4,128,128]{3,2,1,0:T(8,128)S(1)}, f32[8,4,128,128]{3,2,1,0:T(8,128)}, u32[]{:S(2)}) copy-start(f32[8,4,128,128]{3,2,1,0:T(8,128)} %param.8) | copy-start | bytes 6291460
  3.2 16.6 %collective-permute-start = (f32[8,2,128,128]{3,2,1,0:T(8,128)}, f32[8,2,128,128]{3,2,1,0:T(8,128)}, u32[]{:S(2)}, u32[]{:S(2)}) collective-permute-start(f32[8,2,128,128]{3,2,1,0:T(8,128)} %get-tuple-element.11), channel_id=1, source_target_pairs={{0,2},{2,4},{4,6},{6,8},{8,10},{10,12},{12,14},{14,16},{16,18},{18... | collective-permute-start | bytes 3145736 | tf_op jit(solution)/shard_map/ppermute | solution.py:12
  5.2 17.6 %collective-permute-start.1 = (f32[8,2,128,128]{3,2,1,0:T(8,128)}, f32[8,2,128,128]{3,2,1,0:T(8,128)S(1)}, u32[]{:S(2)}, u32[]{:S(2)}) collective-permute-start(f32[8,2,128,128]{3,2,1,0:T(8,128)} %get-tuple-element.12), channel_id=1, source_target_pairs={{2,0},{4,2},{6,4},{8,6},{10,8},{12,10},{14,12},{16,14},{18,16},{20... | collective-permute-start | bytes 3145736 | tf_op jit(solution)/shard_map/ppermute | solution.py:15
  28.4 5.2 %copy-start.3 = (f32[32,16,16]{0,2,1:T(8,128)S(1)}, f32[32,16,16]{0,2,1:T(8,128)}, u32[]{:S(2)}) copy-start(f32[32,16,16]{0,2,1:T(8,128)} %param.15) | copy-start | bytes 98308
  28.4 5.2 %copy-start.4 = (f32[32,16,16]{0,2,1:T(8,128)S(1)}, f32[32,16,16]{0,2,1:T(8,128)}, u32[]{:S(2)}) copy-start(f32[32,16,16]{0,2,1:T(8,128)} %param.14) | copy-start | bytes 98308
  28.4 31.1 %all-to-all-start = ((f32[8,4,128,128]{3,0,1,2:T(8,128)}), f32[8,4,128,128]{3,0,1,2:T(8,128)}, u32[]{:S(2)}, u32[]{:S(2)}) async-start(f32[8,4,128,128]{3,0,1,2:T(8,128)} %select_select_fusion.1), calls=%async_computation | async-start | bytes 4194304 | tf_op jit(solution)/shard_map/all_to_all | solution.py:76
  100.4 16.1 %collective-permute-start.2 = (f32[8,2,128,128]{3,2,1,0:T(8,128)S(1)}, f32[8,2,128,128]{3,2,1,0:T(8,128)S(1)}, u32[]{:S(2)}, u32[]{:S(2)}) collective-permute-start(f32[8,2,128,128]{3,2,1,0:T(8,128)S(1)} %copy.60), channel_id=1, source_target_pairs={{0,2},{2,4},{4,6},{6,8},{8,10},{10,12},{12,14},{14,16},{16,18},{18... | collective-permute-start | bytes 3145736 | tf_op jit(solution)/shard_map/ppermute | solution.py:12
  102.6 15.9 %collective-permute-start.3 = (f32[8,2,128,128]{3,2,1,0:T(8,128)S(1)}, f32[8,2,128,128]{3,2,1,0:T(8,128)S(1)}, u32[]{:S(2)}, u32[]{:S(2)}) collective-permute-start(f32[8,2,128,128]{3,2,1,0:T(8,128)S(1)} %copy.62), channel_id=1, source_target_pairs={{2,0},{4,2},{6,4},{8,6},{10,8},{12,10},{14,12},{16,14},{18,16},{20... | collective-permute-start | bytes 3145736 | tf_op jit(solution)/shard_map/ppermute | solution.py:15
where the time goes:
time: 188 us
  blocking collectives  84.1 us (45%)
  waiting for transfers between devices  46.1 us (25%)
  starting transfers between devices  16.6 us (9%)
  matrix products  16.4 us (9%)
  local copies, waits for them, and re-layouts  14.2 us (8%)
  other arithmetic  10.2 us (5%)
    all_to_all x1, blocking collectives, body(): again = lax.all_to_all(third, 'ga', split_axis=2, concat_axis=0, tiled=True)  28.5 us
    all_to_all x1, blocking collectives, body(): return lax.all_to_all(fourth, 'ga', split_axis=0, concat_axis=2, tiled=True)  27.9 us
    all_to_all x1, blocking collectives, body(): lax.all_to_all(second, 'ga', split_axis=0, concat_axis=2, tiled=True)  27.7 us
    all_to_all x1, waiting for transfers between devices, body(): lax.all_to_all(first, 'ga', split_axis=2, concat_axis=0, tiled=True)  24.3 us
    ppermute x2, waiting for transfers between devices, padded(): lax.ppermute(lax.slice_in_dim(block, block.shape[dim] - width, None, axis...  20.3 us
    dot_general x2, matrix products, regroup(): lax.dot_general(coeffs, blocks, (((3,), (0,)), ((0, 1), (1, 2))), precisi...  15.8 us
    select_n x2, other arithmetic, advect(): jnp.where(flags[None] == 1, inlet_frac[:, None, None, None] * jnp.ones_li...  7.58 us
    ppermute x2, starting transfers between devices, padded(): lax.ppermute(lax.slice_in_dim(block, 0, width, axis=dim), axis, backward)  7.5 us
  transfers between devices with their start and end apart: 5, of which 4 were waited for; matrix products, arithmetic and copies ran while one was open for 3% of the time, Pallas kernels for 0%

commit v1 on v0

v1 whole, which is shorter than its diff:
```python
import functools

import jax
import jax.numpy as jnp
from jax import lax
from jax.experimental import pallas as pl
from jax.experimental.pallas import tpu as pltpu
from jax.sharding import PartitionSpec as P

CHUNKS = 2
SUB = 8
F32 = jnp.float32
BF16 = jnp.bfloat16


def setup(me, courant, spread, inlet, perm, coef, groups):
    half = groups // 2
    quarter = half // 2
    for role in range(2):
        base = jnp.where(me == role, 0, half)
        npos = jnp.int32(0)
        nneg = jnp.int32(0)
        for g in range(half):
            c = courant[base + g]
            pos = c > 0.0
            slot = jnp.where(pos, role * quarter + npos, half + role * quarter + nneg)
            npos = npos + jnp.where(pos, 1, 0)
            nneg = nneg + jnp.where(pos, 0, 1)
            perm[slot] = role * half + g
            if coef is not None:
                a = jnp.where(pos, c, -c)
                s = spread[base + g]
                coef[0, slot] = 1.0 - 1.5 * a + 0.5 * a * a - 2.0 * s
                coef[1, slot] = 2.0 * a - a * a + s
                coef[2, slot] = 0.5 * a * a - 0.5 * a
                coef[3, slot] = s
                coef[4, slot] = inlet[base + g]


def pack_halo(load, perm, up, down, groups, planes):
    half = groups // 2
    for i in range(half):
        p = perm[i]
        up[2 * i] = load(i, p, planes - 2)
        up[2 * i + 1] = load(i, p, planes - 1)
        down[groups + i] = load(i, p, 0)
        n = perm[half + i]
        up[groups + i] = load(i, n, planes - 1)
        down[2 * i] = load(i, n, 0)
        down[2 * i + 1] = load(i, n, 1)


def halo_kernel(me, courant, own, peer, up, down, perm):
    planes = own.shape[1]
    groups = 2 * own.shape[0]
    half = groups // 2
    quarter = half // 2

    @pl.when(pl.program_id(0) == 0)
    def _():
        setup(me[0], courant, None, None, perm, None, groups)

    def load(i, row, z):
        if i < quarter:
            return own[row, z]
        return peer[row - half, z]

    pack_halo(load, perm, up, down, groups, planes)


def step_kernel(
    chunk, last, me, courant, spread, inlet, tidx, *refs
):
    if last:
        src, low, high, flags, tab, _, keep, send, perm, coef, scr, res = refs
        groups = src.shape[0]
        planes = src.shape[1]
    else:
        own, peer, low, high, flags, tab, second, up, down, perm, coef, scr, res = refs
        groups = 2 * own.shape[0]
        planes = own.shape[1]
    half = groups // 2
    quarter = half // 2
    step = pl.program_id(0)
    rows = planes * SUB

    @pl.when(step == 0)
    def _():
        setup(me[0], courant, spread, inlet, perm, coef, groups)

    wall = [flags[z] == 2 for z in range(planes)]
    entry = [flags[z] == 1 for z in range(planes)]
    for i in range(groups):
        row = perm[i]
        if last:
            f = [src[row, z] for z in range(planes)]
        elif i % half < quarter:
            f = [own[row, z] for z in range(planes)]
        else:
            f = [peer[row - half, z] for z in range(planes)]
        c0, c1, c2, c3, c4 = (coef[k, i] for k in range(5))
        if i < half:
            ext = [low[2 * i], low[2 * i + 1]] + f + [high[groups + i]]
            taps = [(ext[z + 2], ext[z + 1], ext[z], ext[z + 3]) for z in range(planes)]
        else:
            k = i - half
            ext = [low[groups + k]] + f + [high[2 * k], high[2 * k + 1]]
            taps = [(ext[z + 1], ext[z + 2], ext[z + 3], ext[z]) for z in range(planes)]
        for z in range(planes):
            a, b, c, d = taps[z]
            v = (c0 * a + c1 * b) + (c2 * c + c3 * d)
            v = jnp.where(wall[z], 0.0, v)
            v = jnp.where(entry[z], c4, v)
            scr[pl.ds(row * rows + z * SUB, SUB), :] = v

    first_block = me[1] + chunk + step * SUB
    for z in range(planes):
        for b in range(SUB):
            r = z * SUB + b
            x = scr[pl.ds(r, groups, stride=rows), :]
            hi = x.astype(BF16)
            lo = (x - hi.astype(F32)).astype(BF16)
            rhs = jnp.concatenate([hi, hi, lo], axis=0)
            t = tidx[z, first_block + b]
            y = jnp.dot(tab[t], rhs, preferred_element_type=F32)
            out = x + (y[:groups] + x * y[groups:])
            res[pl.ds(r, groups, stride=rows), :] = out

    def done(g, z):
        return res[pl.ds(g * rows + z * SUB, SUB), :]

    if last:
        for g in range(half):
            for z in range(planes):
                keep[g, z] = done(g, z)
                send[g, z] = done(half + g, z)
    else:
        for g in range(groups):
            for z in range(planes):
                second[g, z] = done(g, z)
        pack_halo(lambda i, row, z: done(row, z), perm, up, down, groups, planes)


def smem():
    return pl.BlockSpec(memory_space=pltpu.SMEM)


def body(fractions, courant, spread, inlet_frac, flags, table_index, lin_table, quad_table):
    half, planes, nblk, width = fractions.shape
    groups = 2 * half
    ntab = lin_table.shape[0]
    member = lax.axis_index("ga")
    mine = nblk // 2
    size = mine // CHUNKS
    steps = size // SUB
    nhalo = 3 * half
    count = lax.axis_size("gz")
    forward = [(i, i + 1) for i in range(count - 1)]
    backward = [(b, a) for a, b in forward]
    swap = [(0, 1), (1, 0)]
    own_base = member * mine
    peer_base = (1 - member) * mine
    me = jnp.stack([member, own_base, own_base // SUB, peer_base // SUB]).astype(jnp.int32)

    def tables():
        both = jnp.concatenate([lin_table, quad_table], axis=1) * 0.25
        swapped = jnp.concatenate([both[:, :, half:], both[:, :, :half]], axis=2)
        swapped = jnp.concatenate(
            [swapped[:, half:groups], swapped[:, :half], swapped[:, groups + half:], swapped[:, groups:groups + half]],
            axis=1,
        )
        both = jnp.where(member == 1, swapped, both)
        hi = lax.reduce_precision(both, 8, 7)
        lo = both - hi
        return jnp.concatenate([hi, lo, hi], axis=2).astype(BF16)

    def spec(lead, at=None):
        n = len(lead)

        def index(i, me_ref, c=at):
            return (0,) * n + ((i if c is None else me_ref[2] + c + i), 0)

        return pl.BlockSpec(tuple(lead) + (SUB, width), index)

    def shape(*dims):
        return jax.ShapeDtypeStruct(dims, F32)

    def call(kernel, ins, outs, in_specs, out_specs, scratch, aliases={}, flops=0):
        nbytes = sum(x.size * 4 for x in outs) * 2
        return pl.pallas_call(
            kernel,
            out_shape=outs,
            grid_spec=pltpu.PrefetchScalarGridSpec(
                num_scalar_prefetch=1,
                grid=(steps,),
                in_specs=in_specs,
                out_specs=out_specs,
                scratch_shapes=scratch,
            ),
            input_output_aliases=aliases,
            cost_estimate=pl.CostEstimate(flops=flops, bytes_accessed=nbytes, transcendentals=0),
        )(me, *ins)

    sends = []
    for c in range(CHUNKS):
        sends.append(lax.dynamic_slice_in_dim(fractions, peer_base + c * size, size, axis=2))
    got = [lax.ppermute(x, "ga", swap) for x in sends]
    tab = tables()

    tiles = [
        pltpu.SMEM((groups,), jnp.int32),
    ]
    work = [
        pltpu.SMEM((groups,), jnp.int32),
        pltpu.SMEM((5, groups), F32),
        pltpu.VMEM((groups * planes * SUB, width), F32),
        pltpu.VMEM((groups * planes * SUB, width), F32),
    ]
    tab_spec = pl.BlockSpec((ntab, 2 * groups, 3 * groups), lambda i, m: (0, 0, 0))
    flops = 2 * 2 * groups * 3 * groups * planes * size * width

    out = None
    returned = []
    for c in range(CHUNKS):
        at = c * steps
        halo_spec = spec((nhalo,))
        halo_shape = shape(nhalo, size, width)
        up, down = call(
            halo_kernel,
            (courant, fractions, got[c]),
            (halo_shape, halo_shape),
            [smem(), spec((half, planes), at), spec((half, planes))],
            (halo_spec, halo_spec),
            tiles,
        )
        low = lax.ppermute(up, "gz", forward)
        high = lax.ppermute(down, "gz", backward)
        second, up, down = call(
            functools.partial(step_kernel, c * size, False),
            (courant, spread, inlet_frac, table_index, fractions, got[c], low, high, flags, tab),
            (shape(groups, planes, size, width), halo_shape, halo_shape),
            [smem()] * 4
            + [spec((half, planes), at), spec((half, planes)), halo_spec, halo_spec, spec((planes,), at), tab_spec],
            (spec((groups, planes)), halo_spec, halo_spec),
            work,
            flops=flops,
        )
        low = lax.ppermute(up, "gz", forward)
        high = lax.ppermute(down, "gz", backward)
        prior = jnp.zeros((1,), F32) if out is None else out
        out, send = call(
            functools.partial(step_kernel, c * size, True),
            (courant, spread, inlet_frac, table_index, second, low, high, flags, tab, prior),
            (shape(half, planes, nblk, width), shape(half, planes, size, width)),
            [smem()] * 4
            + [spec((groups, planes)), halo_spec, halo_spec, spec((planes,), at), tab_spec, pl.BlockSpec(memory_space=pl.ANY)],
            (spec((half, planes), at), spec((half, planes))),
            work,
            aliases={} if c == 0 else {10: 0},
            flops=flops,
        )
        returned.append(lax.ppermute(send, "ga", swap))

    def place(block, c):
        def copy(m, src, _, dst):
            dst[...] = src[...]

        return pl.pallas_call(
            copy,
            out_shape=shape(half, planes, nblk, width),
            grid_spec=pltpu.PrefetchScalarGridSpec(
                num_scalar_prefetch=1,
                grid=(steps,),
                in_specs=[spec((half, planes)), pl.BlockSpec(memory_space=pl.ANY)],
                out_specs=pl.BlockSpec(
                    (half, planes, SUB, width), lambda i, m: (0, 0, m[3] + c * steps + i, 0)
                ),
            ),
            input_output_aliases={2: 0},
        )(me, block, out)

    for c in range(CHUNKS):
        out = place(returned[c], c)
    return out


def solution(mesh):
    placed = (
        P("ga", "gz", None, None),
        P(),
        P(),
        P(),
        P("gz", None, None),
        P("gz", None),
        P(),
        P(),
    )
    return jax.shard_map(
        body, mesh=mesh, in_specs=placed, out_specs=P("ga", "gz", None, None), check_vma=False
    )
```

time: 188 us -> 140 us (0.74)
  the two profiles are of different devices: /device:TPU:10 before, /device:TPU:6 now
where the time goes in v1:
time: 140 us; the launch traced here: 139 us
  starting transfers between devices  49.2 us (35%)
  waiting for transfers between devices  39.7 us (28%)
  Pallas kernels  39.1 us (28%)
  local copies, waits for them, and re-layouts  9.09 us (6%)
  other arithmetic  1.97 us (1%)
    ppermute x4, starting transfers between devices, body(): high = lax.ppermute(down, 'gz', backward)  35.7 us
    pallas_call x6, Pallas kernels, call(): pl.pallas_call(kernel, out_shape=outs, grid_spec=pltpu.PrefetchScalarGrid...  31.4 us
    ppermute x2, waiting for transfers between devices, body(): got = [lax.ppermute(x, 'ga', swap) for x in sends]  21.6 us
    ppermute x2, waiting for transfers between devices, body(): returned.append(lax.ppermute(send, 'ga', swap))  7.68 us
    pallas_call x2, Pallas kernels, place(): pl.pallas_call(copy, out_shape=shape(half, planes, nblk, width), grid_spe...  7.65 us
    ppermute x4, starting transfers between devices, body(): low = lax.ppermute(up, 'gz', forward)  7.63 us
    unnamed x28, local copies, waits for them, and re-layouts  6.75 us
    ppermute x4, waiting for transfers between devices, body(): low = lax.ppermute(up, 'gz', forward)  5.54 us
  transfers between devices with their start and end apart: 12, of which 6 were waited for; matrix products, arithmetic and copies ran while one was open for 2% of the time, Pallas kernels for 25%

profile of v1, /device:TPU:6, one launch (start us, length us, event | category | flops | bytes accessed | tf_op | source)
XLA Modules:
  0.0 139.3 jit_solution(18233707076860838625)
XLA Ops:
  0.0 2.1 %constant_dynamic-slice_fusion = (f32[8,4,32,128]{3,2,1,0:T(8,128)S(1)}, f32[8,4,32,128]{3,2,1,0:T(8,128)}) fusion(f32[8,4,128,128]{3,2,1,0:T(8,128)} %refs_0_.3, s32[]{:T(128)S(6)} %select_n.27, s32[]{:T(128)S(6)} %select_n.24), kind=kLoop, calls=%fused_computation.19 | loop fusion | bytes 2097160 | tf_op jit(solution)/shard_map/dynamic_slice | solution.py:206
  2.1 1.9 %collective-permute-start.5 = (f32[8,4,32,128]{3,2,1,0:T(8,128)S(1)}, f32[8,4,32,128]{3,2,1,0:T(8,128)S(1)}, u32[]{:S(2)}, u32[]{:S(2)}) collective-permute-start(f32[8,4,32,128]{3,2,1,0:T(8,128)S(1)} %get-tuple-element.35), channel_id=1, source_target_pairs={{0,1},{1,0},{2,3},{3,2},{4,5},{5,4},{6,7},{7,6},{8,9},{9,8},{10,11... | collective-permute-start | bytes 1572872 | tf_op jit(solution)/shard_map/ppermute | solution.py:207
  5.6 21.6 %collective-permute-done.peer.refs_1_ = f32[8,4,32,128]{3,2,1,0:T(8,128)S(1)} collective-permute-done((f32[8,4,32,128]{3,2,1,0:T(8,128)}, f32[8,4,32,128]{3,2,1,0:T(8,128)S(1)}, u32[]{:S(2)}, u32[]{:S(2)}) %collective-permute-start) | collective-permute-done | bytes 524320 | tf_op jit(solution)/shard_map/ppermute | solution.py:207
  28.0 4.2 %shard_map.82 = (f32[24,32,128]{2,1,0:T(8,128)}, f32[24,32,128]{2,1,0:T(8,128)}) custom-call(s32[4]{0:T(128)} %pad_add_fusion.me.m, f32[16]{0:T(128)} %courant.11, f32[8,4,128,128]{3,2,1,0:T(8,128)} %refs_0_.3, f32[8,4,32,128]{3,2,1,0:T(8,128)} %copy-done), custom_call_target="tpu_custom_call" | custom-call | bytes 1572864 | tf_op jit(solution)/shard_map/pallas_call | solution.py:190
  32.2 1.9 %collective-permute-start.1 = (f32[24,32,128]{2,1,0:T(8,128)}, f32[24,32,128]{2,1,0:T(8,128)S(1)}, u32[]{:S(2)}, u32[]{:S(2)}) collective-permute-start(f32[24,32,128]{2,1,0:T(8,128)} %get-tuple-element.19), channel_id=1, source_target_pairs={{0,2},{2,4},{4,6},{6,8},{8,10},{10,12},{12,14},{14,16},{16,18},{18... | collective-permute-start | bytes 1179656 | tf_op jit(solution)/shard_map/ppermute | solution.py:236
  34.1 9.3 %collective-permute-start.2 = (f32[24,32,128]{2,1,0:T(8,128)}, f32[24,32,128]{2,1,0:T(8,128)}, u32[]{:S(2)}, u32[]{:S(2)}) collective-permute-start(f32[24,32,128]{2,1,0:T(8,128)} %get-tuple-element.20), channel_id=1, source_target_pairs={{2,0},{4,2},{6,4},{8,6},{10,8},{12,10},{14,12},{16,14},{18,16},{20... | collective-permute-start | bytes 1179656 | tf_op jit(solution)/shard_map/ppermute | solution.py:237
  44.2 4.2 %shard_map.84 = (f32[24,32,128]{2,1,0:T(8,128)}, f32[24,32,128]{2,1,0:T(8,128)}) custom-call(s32[4]{0:T(128)} %pad_add_fusion.me.m, f32[16]{0:T(128)} %courant.11, f32[8,4,128,128]{3,2,1,0:T(8,128)} %refs_0_.3, f32[8,4,32,128]{3,2,1,0:T(8,128)} %copy-done.1), custom_call_target="tpu_custom_call" | custom-call | bytes 1572864 | tf_op jit(solution)/shard_map/pallas_call | solution.py:190
  48.4 1.9 %collective-permute-start.6 = (f32[24,32,128]{2,1,0:T(8,128)}, f32[24,32,128]{2,1,0:T(8,128)S(1)}, u32[]{:S(2)}, u32[]{:S(2)}) collective-permute-start(f32[24,32,128]{2,1,0:T(8,128)} %get-tuple-element.24), channel_id=1, source_target_pairs={{0,2},{2,4},{4,6},{6,8},{8,10},{10,12},{12,14},{14,16},{16,18},{18... | collective-permute-start | bytes 1179656 | tf_op jit(solution)/shard_map/ppermute | solution.py:236
  50.3 8.8 %collective-permute-start.7 = (f32[24,32,128]{2,1,0:T(8,128)}, f32[24,32,128]{2,1,0:T(8,128)S(1)}, u32[]{:S(2)}, u32[]{:S(2)}) collective-permute-start(f32[24,32,128]{2,1,0:T(8,128)} %get-tuple-element.25), channel_id=1, source_target_pairs={{2,0},{4,2},{6,4},{8,6},{10,8},{12,10},{14,12},{16,14},{18,16},{20... | collective-permute-start | bytes 1179656 | tf_op jit(solution)/shard_map/ppermute | solution.py:237
  60.3 3.8 %collective-permute-done.6.refs_2_ = f32[24,32,128]{2,1,0:T(8,128)S(1)} collective-permute-done((f32[24,32,128]{2,1,0:T(8,128)}, f32[24,32,128]{2,1,0:T(8,128)S(1)}, u32[]{:S(2)}, u32[]{:S(2)}) %collective-permute-start.6) | collective-permute-done | bytes 393248 | tf_op jit(solution)/shard_map/ppermute | solution.py:236
  64.1 4.8 %collective-permute-done.7.refs_3_ = f32[24,32,128]{2,1,0:T(8,128)S(1)} collective-permute-done((f32[24,32,128]{2,1,0:T(8,128)}, f32[24,32,128]{2,1,0:T(8,128)S(1)}, u32[]{:S(2)}, u32[]{:S(2)}) %collective-permute-start.7) | collective-permute-done | bytes 393248 | tf_op jit(solution)/shard_map/ppermute | solution.py:237
  69.7 6.0 %shard_map.85 = (f32[16,4,32,128]{3,2,1,0:T(8,128)}, f32[24,32,128]{2,1,0:T(8,128)}, f32[24,32,128]{2,1,0:T(8,128)}) custom-call(s32[4]{0:T(128)} %pad_add_fusion.me.m, f32[16]{0:T(128)} %courant.11, f32[16]{0:T(128)} %spread.7, f32[16]{0:T(128)} %inlet.7, s32[4,128]{1,0:T(4,128)} %tidx.7, f32[8,4,128,128]{3,2,1,0:T(8,128)} %refs_0_.3, ...), custom_call_target="tpu_custom_call" | custom-call | flops 50331648 | bytes 3670016 | tf_op jit(solution)/shard_map/pallas_call | solution.py:190
  75.7 1.9 %collective-permute-start.8 = (f32[24,32,128]{2,1,0:T(8,128)}, f32[24,32,128]{2,1,0:T(8,128)S(1)}, u32[]{:S(2)}, u32[]{:S(2)}) collective-permute-start(f32[24,32,128]{2,1,0:T(8,128)} %get-tuple-element.27), channel_id=1, source_target_pairs={{0,2},{2,4},{4,6},{6,8},{8,10},{10,12},{12,14},{14,16},{16,18},{18... | collective-permute-start | bytes 1179656 | tf_op jit(solution)/shard_map/ppermute | solution.py:248
  77.6 8.8 %collective-permute-start.9 = (f32[24,32,128]{2,1,0:T(8,128)}, f32[24,32,128]{2,1,0:T(8,128)S(1)}, u32[]{:S(2)}, u32[]{:S(2)}) collective-permute-start(f32[24,32,128]{2,1,0:T(8,128)} %get-tuple-element.28), channel_id=1, source_target_pairs={{2,0},{4,2},{6,4},{8,6},{10,8},{12,10},{14,12},{16,14},{18,16},{20... | collective-permute-start | bytes 1179656 | tf_op jit(solution)/shard_map/ppermute | solution.py:249
  87.2 5.9 %shard_map.83 = (f32[16,4,32,128]{3,2,1,0:T(8,128)}, f32[24,32,128]{2,1,0:T(8,128)}, f32[24,32,128]{2,1,0:T(8,128)}) custom-call(s32[4]{0:T(128)} %pad_add_fusion.me.m, f32[16]{0:T(128)} %courant.11, f32[16]{0:T(128)} %spread.7, f32[16]{0:T(128)} %inlet.7, s32[4,128]{1,0:T(4,128)} %tidx.7, f32[8,4,128,128]{3,2,1,0:T(8,128)} %refs_0_.3, ...), custom_call_target="tpu_custom_call" | custom-call | flops 50331648 | bytes 3670016 | tf_op jit(solution)/shard_map/pallas_call | solution.py:190
  93.1 1.9 %collective-permute-start.3 = (f32[24,32,128]{2,1,0:T(8,128)}, f32[24,32,128]{2,1,0:T(8,128)S(1)}, u32[]{:S(2)}, u32[]{:S(2)}) collective-permute-start(f32[24,32,128]{2,1,0:T(8,128)} %get-tuple-element.22), channel_id=1, source_target_pairs={{0,2},{2,4},{4,6},{6,8},{8,10},{10,12},{12,14},{14,16},{16,18},{18... | collective-permute-start | bytes 1179656 | tf_op jit(solution)/shard_map/ppermute | solution.py:248
  95.0 8.8 %collective-permute-start.4 = (f32[24,32,128]{2,1,0:T(8,128)}, f32[24,32,128]{2,1,0:T(8,128)S(1)}, u32[]{:S(2)}, u32[]{:S(2)}) collective-permute-start(f32[24,32,128]{2,1,0:T(8,128)} %get-tuple-element.23), channel_id=1, source_target_pairs={{2,0},{4,2},{6,4},{8,6},{10,8},{12,10},{14,12},{16,14},{18,16},{20... | collective-permute-start | bytes 1179656 | tf_op jit(solution)/shard_map/ppermute | solution.py:249
  104.7 5.6 %shard_map.86 = (f32[8,4,128,128]{3,2,1,0:T(8,128)}, f32[8,4,32,128]{3,2,1,0:T(8,128)}) custom-call(s32[4]{0:T(128)} %pad_add_fusion.me.m, f32[16]{0:T(128)} %courant.11, f32[16]{0:T(128)} %spread.7, f32[16]{0:T(128)} %inlet.7, s32[4,128]{1,0:T(4,128)} %tidx.7, f32[16,4,32,128]{3,2,1,0:T(8,128)} %get-tuple-element.26.refs_0_, f32[24,32,128]{2,1,0:T(8,128)} %copy-done.9, ...), custom_call_target="tpu_custom_call" | custom-call | flops 50331648 | bytes 5242880 | tf_op jit(solution)/shard_map/pallas_call | solution.py:190
  112.9 5.6 %shard_map.87 = (f32[8,4,128,128]{3,2,1,0:T(8,128)}, f32[8,4,32,128]{3,2,1,0:T(8,128)}) custom-call(s32[4]{0:T(128)} %pad_add_fusion.me.m, f32[16]{0:T(128)} %courant.11, f32[16]{0:T(128)} %spread.7, f32[16]{0:T(128)} %inlet.7, s32[4,128]{1,0:T(4,128)} %tidx.7, f32[16,4,32,128]{3,2,1,0:T(8,128)} %get-tuple-element.21.refs_0_, ...), custom_call_target="tpu_custom_call", output_to_operand_aliasing={{0}: (10, {})} | custom-call | flops 50331648 | bytes 5242880 | tf_op jit(solution)/shard_map/pallas_call | solution.py:190
  118.5 3.8 %collective-permute-start.10 = (f32[8,4,32,128]{3,2,1,0:T(8,128)}, f32[8,4,32,128]{3,2,1,0:T(8,128)S(1)}, u32[]{:S(2)}, u32[]{:S(2)}) collective-permute-start(f32[8,4,32,128]{3,2,1,0:T(8,128)} %get-tuple-element.30), channel_id=1, source_target_pairs={{0,1},{1,0},{2,3},{3,2},{4,5},{5,4},{6,7},{7,6},{8,9},{9,8},{10,11... | collective-permute-start | bytes 1572872 | tf_op jit(solution)/shard_map/ppermute | solution.py:262
  122.4 5.2 %collective-permute-done.11.src = f32[8,4,32,128]{3,2,1,0:T(8,128)S(1)} collective-permute-done((f32[8,4,32,128]{3,2,1,0:T(8,128)}, f32[8,4,32,128]{3,2,1,0:T(8,128)S(1)}, u32[]{:S(2)}, u32[]{:S(2)}) %collective-permute-start.11) | collective-permute-done | bytes 524320 | tf_op jit(solution)/shard_map/ppermute | solution.py:262
  128.4 3.8 %shard_map.88._ = f32[8,4,128,128]{3,2,1,0:T(8,128)} custom-call(s32[4]{0:T(128)} %pad_add_fusion.me.m, f32[8,4,32,128]{3,2,1,0:T(8,128)} %copy-done.2, f32[8,4,128,128]{3,2,1,0:T(8,128)} %get-tuple-element.32._), custom_call_target="tpu_custom_call", output_to_operand_aliasing={{}: (2, {})} | custom-call | tf_op jit(solution)/shard_map/pallas_call | solution.py:268
  132.2 2.5 %collective-permute-done.10.src = f32[8,4,32,128]{3,2,1,0:T(8,128)S(1)} collective-permute-done((f32[8,4,32,128]{3,2,1,0:T(8,128)}, f32[8,4,32,128]{3,2,1,0:T(8,128)S(1)}, u32[]{:S(2)}, u32[]{:S(2)}) %collective-permute-start.10) | collective-permute-done | bytes 524320 | tf_op jit(solution)/shard_map/ppermute | solution.py:262
  135.5 3.8 %shard_map.89 = f32[8,4,128,128]{3,2,1,0:T(8,128)} custom-call(s32[4]{0:T(128)} %pad_add_fusion.me.m, f32[8,4,32,128]{3,2,1,0:T(8,128)} %copy-done.3, f32[8,4,128,128]{3,2,1,0:T(8,128)} %shard_map.88._), custom_call_target="tpu_custom_call", output_to_operand_aliasing={{}: (2, {})} | custom-call | tf_op jit(solution)/shard_map/pallas_call | solution.py:268
  (44 shorter events, 10.8 us)
Async XLA Ops:
  0.0 4.7 %copy-start.11 = (f32[32,16,16]{0,2,1:T(8,128)S(1)}, f32[32,16,16]{0,2,1:T(8,128)}, u32[]{:S(2)}) copy-start(f32[32,16,16]{0,2,1:T(8,128)} %param.14) | copy-start | bytes 98308
  0.0 4.9 %copy-start.12 = (f32[32,16,16]{0,2,1:T(8,128)S(1)}, f32[32,16,16]{0,2,1:T(8,128)}, u32[]{:S(2)}) copy-start(f32[32,16,16]{0,2,1:T(8,128)} %param.15) | copy-start | bytes 98308
  2.1 41.3 %collective-permute-start.5 = (f32[8,4,32,128]{3,2,1,0:T(8,128)S(1)}, f32[8,4,32,128]{3,2,1,0:T(8,128)S(1)}, u32[]{:S(2)}, u32[]{:S(2)}) collective-permute-start(f32[8,4,32,128]{3,2,1,0:T(8,128)S(1)} %get-tuple-element.35), channel_id=1, source_target_pairs={{0,1},{1,0},{2,3},{3,2},{4,5},{5,4},{6,7},{7,6},{8,9},{9,8},{10,11... | collective-permute-start | bytes 1572872 | tf_op jit(solution)/shard_map/ppermute | solution.py:207
  4.1 23.2 %collective-permute-start = (f32[8,4,32,128]{3,2,1,0:T(8,128)}, f32[8,4,32,128]{3,2,1,0:T(8,128)S(1)}, u32[]{:S(2)}, u32[]{:S(2)}) collective-permute-start(f32[8,4,32,128]{3,2,1,0:T(8,128)} %get-tuple-element.36), channel_id=1, source_target_pairs={{0,1},{1,0},{2,3},{3,2},{4,5},{5,4},{6,7},{7,6},{8,9},{9,8},{10,11... | collective-permute-start | bytes 1572872 | tf_op jit(solution)/shard_map/ppermute | solution.py:207
  27.2 0.8 copy-start
  32.2 54.2 %collective-permute-start.1 = (f32[24,32,128]{2,1,0:T(8,128)}, f32[24,32,128]{2,1,0:T(8,128)S(1)}, u32[]{:S(2)}, u32[]{:S(2)}) collective-permute-start(f32[24,32,128]{2,1,0:T(8,128)} %get-tuple-element.19), channel_id=1, source_target_pairs={{0,2},{2,4},{4,6},{6,8},{8,10},{10,12},{12,14},{14,16},{16,18},{18... | collective-permute-start | bytes 1179656 | tf_op jit(solution)/shard_map/ppermute | solution.py:236
  34.1 52.3 %collective-permute-start.2 = (f32[24,32,128]{2,1,0:T(8,128)}, f32[24,32,128]{2,1,0:T(8,128)}, u32[]{:S(2)}, u32[]{:S(2)}) collective-permute-start(f32[24,32,128]{2,1,0:T(8,128)} %get-tuple-element.20), channel_id=1, source_target_pairs={{2,0},{4,2},{6,4},{8,6},{10,8},{12,10},{14,12},{16,14},{18,16},{20... | collective-permute-start | bytes 1179656 | tf_op jit(solution)/shard_map/ppermute | solution.py:237
  43.4 0.8 copy-start.1
  48.4 15.7 %collective-permute-start.6 = (f32[24,32,128]{2,1,0:T(8,128)}, f32[24,32,128]{2,1,0:T(8,128)S(1)}, u32[]{:S(2)}, u32[]{:S(2)}) collective-permute-start(f32[24,32,128]{2,1,0:T(8,128)} %get-tuple-element.24), channel_id=1, source_target_pairs={{0,2},{2,4},{4,6},{6,8},{8,10},{10,12},{12,14},{14,16},{16,18},{18... | collective-permute-start | bytes 1179656 | tf_op jit(solution)/shard_map/ppermute | solution.py:236
  50.3 18.6 %collective-permute-start.7 = (f32[24,32,128]{2,1,0:T(8,128)}, f32[24,32,128]{2,1,0:T(8,128)S(1)}, u32[]{:S(2)}, u32[]{:S(2)}) collective-permute-start(f32[24,32,128]{2,1,0:T(8,128)} %get-tuple-element.25), channel_id=1, source_target_pairs={{2,0},{4,2},{6,4},{8,6},{10,8},{12,10},{14,12},{16,14},{18,16},{20... | collective-permute-start | bytes 1179656 | tf_op jit(solution)/shard_map/ppermute | solution.py:237
  64.1 4.8 %copy-start.6 = (f32[24,32,128]{2,1,0:T(8,128)}, f32[24,32,128]{2,1,0:T(8,128)S(1)}, u32[]{:S(2)}) copy-start(f32[24,32,128]{2,1,0:T(8,128)S(1)} %collective-permute-done.6.refs_2_) | copy-start | bytes 1179652
  68.9 0.8 copy-start.8
  75.7 28.1 %collective-permute-start.8 = (f32[24,32,128]{2,1,0:T(8,128)}, f32[24,32,128]{2,1,0:T(8,128)S(1)}, u32[]{:S(2)}, u32[]{:S(2)}) collective-permute-start(f32[24,32,128]{2,1,0:T(8,128)} %get-tuple-element.27), channel_id=1, source_target_pairs={{0,2},{2,4},{4,6},{6,8},{8,10},{10,12},{12,14},{14,16},{16,18},{18... | collective-permute-start | bytes 1179656 | tf_op jit(solution)/shard_map/ppermute | solution.py:248
  77.6 26.2 %collective-permute-start.9 = (f32[24,32,128]{2,1,0:T(8,128)}, f32[24,32,128]{2,1,0:T(8,128)S(1)}, u32[]{:S(2)}, u32[]{:S(2)}) collective-permute-start(f32[24,32,128]{2,1,0:T(8,128)} %get-tuple-element.28), channel_id=1, source_target_pairs={{2,0},{4,2},{6,4},{8,6},{10,8},{12,10},{14,12},{16,14},{18,16},{20... | collective-permute-start | bytes 1179656 | tf_op jit(solution)/shard_map/ppermute | solution.py:249
  86.4 0.8 copy-start.4
  93.1 18.9 %collective-permute-start.3 = (f32[24,32,128]{2,1,0:T(8,128)}, f32[24,32,128]{2,1,0:T(8,128)S(1)}, u32[]{:S(2)}, u32[]{:S(2)}) collective-permute-start(f32[24,32,128]{2,1,0:T(8,128)} %get-tuple-element.22), channel_id=1, source_target_pairs={{0,2},{2,4},{4,6},{6,8},{8,10},{10,12},{12,14},{14,16},{16,18},{18... | collective-permute-start | bytes 1179656 | tf_op jit(solution)/shard_map/ppermute | solution.py:248
  95.0 17.0 %collective-permute-start.4 = (f32[24,32,128]{2,1,0:T(8,128)}, f32[24,32,128]{2,1,0:T(8,128)S(1)}, u32[]{:S(2)}, u32[]{:S(2)}) collective-permute-start(f32[24,32,128]{2,1,0:T(8,128)} %get-tuple-element.23), channel_id=1, source_target_pairs={{2,0},{4,2},{6,4},{8,6},{10,8},{12,10},{14,12},{16,14},{18,16},{20... | collective-permute-start | bytes 1179656 | tf_op jit(solution)/shard_map/ppermute | solution.py:249
  103.8 0.9 copy-start.10
  110.2 17.3 %collective-permute-start.11 = (f32[8,4,32,128]{3,2,1,0:T(8,128)}, f32[8,4,32,128]{3,2,1,0:T(8,128)S(1)}, u32[]{:S(2)}, u32[]{:S(2)}) collective-permute-start(f32[8,4,32,128]{3,2,1,0:T(8,128)} %get-tuple-element.31), channel_id=1, source_target_pairs={{0,1},{1,0},{2,3},{3,2},{4,5},{5,4},{6,7},{7,6},{8,9},{9,8},{10,11... | collective-permute-start | bytes 1572872 | tf_op jit(solution)/shard_map/ppermute | solution.py:262
  112.0 0.7 copy-start.5
  112.0 0.9 copy-start.7
  118.5 16.1 %collective-permute-start.10 = (f32[8,4,32,128]{3,2,1,0:T(8,128)}, f32[8,4,32,128]{3,2,1,0:T(8,128)S(1)}, u32[]{:S(2)}, u32[]{:S(2)}) collective-permute-start(f32[8,4,32,128]{3,2,1,0:T(8,128)} %get-tuple-element.30), channel_id=1, source_target_pairs={{0,1},{1,0},{2,3},{3,2},{4,5},{5,4},{6,7},{7,6},{8,9},{9,8},{10,11... | collective-permute-start | bytes 1572872 | tf_op jit(solution)/shard_map/ppermute | solution.py:262
  127.6 0.8 copy-start.2
  134.7 0.8 copy-start.3
  (1 other events, 0.7 us)
